TPU v7x, 32 devices: a whole 2x2x4 slice. The times are simulated.
32 devices in a mesh: dp: 8 (over y, x, core), tensor: 4 (over z).
Axes of the slice: x: 2, y: 2, z: 4, core: 2. Of those that a mesh axis runs over, the one named last changes fastest.
Arguments:
- target: bfloat16 [8192, 768], P('dp'), may hold values from -6 to 6
- memory: bfloat16 [8192, 768], P('dp'), may hold values from -6 to 6
- target_segments: int32 [8, 1024], P('dp'), may hold values from 0 to 4, as said below
- memory_segments: int32 [8, 1024], P('dp'), may hold values from 0 to 4, as said below
- self_query: bfloat16 [768, 768], P(None, 'tensor'), may hold values from -0.21875 to 0.21875
- self_query_bias: float32 [768], P('tensor'), may hold values from -3 to 3
- self_key: bfloat16 [768, 768], P(None, 'tensor'), may hold values from -0.21875 to 0.21875
- self_value: bfloat16 [768, 768], P(None, 'tensor'), may hold values from -0.21875 to 0.21875
- self_value_bias: float32 [768], P('tensor'), may hold values from -3 to 3
- self_output: bfloat16 [768, 768], P('tensor'), may hold values from -1.25 to 1.25
- self_output_bias: float32 [768], replicated, may hold values from -2 to 2
- first_gain: float32 [768], replicated, may hold values from 0.25 to 1.75
- first_shift: float32 [768], replicated, may hold values from -2 to 2
- cross_query: bfloat16 [768, 768], P(None, 'tensor'), may hold values from -0.21875 to 0.21875
- cross_query_bias: float32 [768], P('tensor'), may hold values from -3 to 3
- cross_key: bfloat16 [768, 768], P(None, 'tensor'), may hold values from -0.21875 to 0.21875
- cross_value: bfloat16 [768, 768], P(None, 'tensor'), may hold values from -0.21875 to 0.21875
- cross_value_bias: float32 [768], P('tensor'), may hold values from -3 to 3
- cross_output: bfloat16 [768, 768], P('tensor'), may hold values from -1.75 to 1.75
- cross_output_bias: float32 [768], replicated, may hold values from -2 to 2
- second_gain: float32 [768], replicated, may hold values from 0.25 to 1.75
- second_shift: float32 [768], replicated, may hold values from -2 to 2
- expand_weight: bfloat16 [768, 3072], P(None, 'tensor'), may hold values from -0.21875 to 0.21875
- expand_bias: float32 [3072], P('tensor'), may hold values from -3 to 3
- contract_weight: bfloat16 [3072, 768], P('tensor'), may hold values from -0.21875 to 0.21875
- contract_bias: float32 [768], replicated, may hold values from -2 to 2
- third_gain: float32 [768], replicated, may hold values from 0.25 to 1.75
- third_shift: float32 [768], replicated, may hold values from -2 to 2
- output_grad: bfloat16 [8192, 768], P('dp'), may hold values from -6 to 6
Outputs:
- layer_output: bfloat16 [8192, 768], P('dp')
- target_grad: bfloat16 [8192, 768], P('dp', 'tensor')
- memory_grad: bfloat16 [8192, 768], P('dp', 'tensor')
- grad_self_query: float32 [768, 768], P('dp', 'tensor')
- grad_self_query_bias: float32 [768], P('tensor')
- grad_self_key: float32 [768, 768], P('dp', 'tensor')
- grad_self_value: float32 [768, 768], P('dp', 'tensor')
- grad_self_value_bias: float32 [768], P('tensor')
- grad_self_output: float32 [768, 768], P('tensor', 'dp')
- grad_self_output_bias: float32 [768], replicated
- grad_first_gain: float32 [768], replicated
- grad_first_shift: float32 [768], replicated
- grad_cross_query: float32 [768, 768], P('dp', 'tensor')
- grad_cross_query_bias: float32 [768], P('tensor')
- grad_cross_key: float32 [768, 768], P('dp', 'tensor')
- grad_cross_value: float32 [768, 768], P('dp', 'tensor')
- grad_cross_value_bias: float32 [768], P('tensor')
- grad_cross_output: float32 [768, 768], P('tensor', 'dp')
- grad_cross_output_bias: float32 [768], replicated
- grad_second_gain: float32 [768], replicated
- grad_second_shift: float32 [768], replicated
- grad_expand_weight: float32 [768, 3072], P('dp', 'tensor')
- grad_expand_bias: float32 [3072], P('tensor')
- grad_contract_weight: float32 [3072, 768], P('tensor', 'dp')
- grad_contract_bias: float32 [768], replicated
- grad_third_gain: float32 [768], replicated
- grad_third_shift: float32 [768], replicated
Inputs may be any that keep to these rules, and one draw needn't show every extreme that they name: `target_segments`: along each row the ids never fall. Ids 0 to 3 are documents, every one present in every row with one or more positions; id 4 marks the padding at the row's end, 1 to 128 positions, and appears in every row. `memory_segments`: same law as target_segments, drawn independently: document d of a memory row belongs to document d of the same target row, and padding of target rows reads padding of memory rows.
All inputs are finite; a program needn't handle non-finite values.
Results may differ from a plain program's by a relative error of at most 0.025.
The roundings to bfloat16 on the way count: a program that leaves them out, or rounds other values in their place, can miss the bound.
Values sent between devices are 32-bit elements; how exact they have to be, the bound alone decides.
A program may use at most 128 MiB of HBM per device.

v0:
```python
from functools import partial

import jax
import jax.numpy as jnp
from jax import lax
from jax.sharding import PartitionSpec as P

HEAD_DIM = 64


EPSILON = 1e-05
NEGATIVE = -1e30


def normalize(summed, norm_gain, norm_shift):
    center = jnp.mean(summed, axis=-1, keepdims=True)
    centered = summed - center
    spread = jnp.mean(centered * centered, axis=-1, keepdims=True)
    return centered * lax.rsqrt(spread + EPSILON) * norm_gain + norm_shift


def exact_gelu(values):
    return jax.nn.gelu(values, approximate=False)


def matmul(left_side, right_side):
    return jnp.dot(left_side, right_side, preferred_element_type=jnp.float32)


def contract_rows(left_side, right_side):
    return lax.dot_general(
        left_side, right_side, (((0,), (0,)), ((), ())), preferred_element_type=jnp.float32
    )


def times_transpose(left_side, right_side):
    return lax.dot_general(
        left_side, right_side, (((1,), (1,)), ((), ())), preferred_element_type=jnp.float32
    )


def column_sums(values):
    return jnp.sum(values.astype(jnp.float32), axis=0)


def block_scores(chosen, key_rows, chosen_ids, key_ids, first_row, causal):
    block_rows = chosen.shape[0]
    allowed = chosen_ids[:, None] == key_ids[None, :]
    if causal:
        query_pos = first_row + jnp.arange(block_rows, dtype=jnp.int32)
        key_pos = jnp.arange(key_rows.shape[0], dtype=jnp.int32)
        allowed = allowed & (query_pos[:, None] >= key_pos[None, :])
    scores = jnp.einsum(
        "qhd,khd->hqk", chosen, key_rows, preferred_element_type=jnp.float32
    ) * chosen.shape[2] ** (-0.5)
    return jnp.where(allowed[None], scores, NEGATIVE)


def attend_row(causal, items):
    query_rows, key_rows, value_rows, query_ids, key_ids = items
    length = query_rows.shape[0]
    block_rows = min(512, length)

    def one_block(block_index):
        first_row = block_index * block_rows
        chosen = lax.dynamic_slice_in_dim(query_rows, first_row, block_rows, 0)
        chosen_ids = lax.dynamic_slice_in_dim(query_ids, first_row, block_rows, 0)
        scores = block_scores(chosen, key_rows, chosen_ids, key_ids, first_row, causal)
        row_max = jnp.max(scores, axis=-1, keepdims=True)
        exponent = jnp.exp(scores - row_max)
        row_sum = jnp.sum(exponent, axis=-1, keepdims=True)
        weights_low = (exponent / row_sum).astype(jnp.bfloat16)
        mixture = jnp.einsum(
            "hqk,khd->qhd", weights_low, value_rows, preferred_element_type=jnp.float32
        )
        return (mixture.astype(jnp.bfloat16), (row_max + jnp.log(row_sum))[..., 0])

    mixture, log_sums = lax.map(one_block, jnp.arange(length // block_rows, dtype=jnp.int32))
    return (mixture.reshape(query_rows.shape), log_sums)


def attend_back(causal, items):
    query_rows, key_rows, value_rows, query_ids, key_ids, log_sums, grad_mixture = items
    length = query_rows.shape[0]
    block_rows = min(512, length)
    score_scale = query_rows.shape[2] ** (-0.5)

    def one_block(carry, block_items):
        block_index, block_sums = block_items
        key_accum, value_accum = carry
        first_row = block_index * block_rows
        chosen = lax.dynamic_slice_in_dim(query_rows, first_row, block_rows, 0)
        chosen_ids = lax.dynamic_slice_in_dim(query_ids, first_row, block_rows, 0)
        chosen_grad = lax.dynamic_slice_in_dim(grad_mixture, first_row, block_rows, 0)
        scores = block_scores(chosen, key_rows, chosen_ids, key_ids, first_row, causal)
        weights_soft = jnp.exp(scores - block_sums[..., None])
        weights_low = weights_soft.astype(jnp.bfloat16)
        grad_weights = jnp.einsum(
            "qhd,khd->hqk", chosen_grad, value_rows, preferred_element_type=jnp.float32
        )
        row_dot = jnp.sum(weights_soft * grad_weights, axis=-1, keepdims=True)
        grad_scores = (weights_soft * (grad_weights - row_dot)).astype(jnp.bfloat16)
        grad_chosen = (
            jnp.einsum("hqk,khd->qhd", grad_scores, key_rows, preferred_element_type=jnp.float32)
            * score_scale
        )
        key_accum = (
            key_accum
            + jnp.einsum("hqk,qhd->khd", grad_scores, chosen, preferred_element_type=jnp.float32)
            * score_scale
        )
        value_accum = value_accum + jnp.einsum(
            "hqk,qhd->khd", weights_low, chosen_grad, preferred_element_type=jnp.float32
        )
        return ((key_accum, value_accum), grad_chosen.astype(jnp.bfloat16))

    zeros_start = jnp.zeros(key_rows.shape, jnp.float32)
    carried, grad_blocks = lax.scan(
        one_block,
        (zeros_start, zeros_start),
        (jnp.arange(length // block_rows, dtype=jnp.int32), log_sums),
    )
    return (
        grad_blocks.reshape(query_rows.shape),
        carried[0].astype(jnp.bfloat16),
        carried[1].astype(jnp.bfloat16),
    )


def per_device(
    target,
    memory,
    target_segments,
    memory_segments,
    self_query,
    self_query_bias,
    self_key,
    self_value,
    self_value_bias,
    self_output,
    self_output_bias,
    first_gain,
    first_shift,
    cross_query,
    cross_query_bias,
    cross_key,
    cross_value,
    cross_value_bias,
    cross_output,
    cross_output_bias,
    second_gain,
    second_shift,
    expand_weight,
    expand_bias,
    contract_weight,
    contract_bias,
    third_gain,
    third_shift,
    output_grad,
):
    row_count = target_segments.shape[0]
    local_width = self_query.shape[1]
    head_count = local_width // HEAD_DIM

    def to_heads(matrix):
        return matrix.reshape(row_count, -1, head_count, HEAD_DIM)

    def to_tokens(stacked):
        return stacked.reshape(-1, local_width)

    def branch_total(partial_term):
        return lax.psum(partial_term, "tensor")

    def input_total(partial_term):
        return lax.psum(partial_term, "tensor")

    def edge_total(partial_term):
        return lax.psum_scatter(partial_term, "tensor", scatter_dimension=1, tiled=True)

    self_queries = (matmul(target, self_query) + self_query_bias).astype(jnp.bfloat16)
    self_keys = matmul(target, self_key).astype(jnp.bfloat16)
    self_values = (matmul(target, self_value) + self_value_bias).astype(jnp.bfloat16)
    self_mixture, self_sums = lax.map(
        partial(attend_row, True),
        (
            to_heads(self_queries),
            to_heads(self_keys),
            to_heads(self_values),
            target_segments,
            target_segments,
        ),
    )
    self_mixed = to_tokens(self_mixture)
    self_branch = branch_total(matmul(self_mixed, self_output)) + self_output_bias
    first_norm, first_back = jax.vjp(
        normalize, target.astype(jnp.float32) + self_branch, first_gain, first_shift
    )
    first_low = first_norm.astype(jnp.bfloat16)
    cross_queries = (matmul(first_low, cross_query) + cross_query_bias).astype(jnp.bfloat16)
    cross_keys = matmul(memory, cross_key).astype(jnp.bfloat16)
    cross_values = (matmul(memory, cross_value) + cross_value_bias).astype(jnp.bfloat16)
    cross_mixture, cross_sums = lax.map(
        partial(attend_row, False),
        (
            to_heads(cross_queries),
            to_heads(cross_keys),
            to_heads(cross_values),
            target_segments,
            memory_segments,
        ),
    )
    cross_mixed = to_tokens(cross_mixture)
    cross_branch = branch_total(matmul(cross_mixed, cross_output)) + cross_output_bias
    second_norm, second_back = jax.vjp(
        normalize, first_norm + cross_branch, second_gain, second_shift
    )
    second_low = second_norm.astype(jnp.bfloat16)
    hidden = matmul(second_low, expand_weight) + expand_bias
    activated_float, gelu_back = jax.vjp(exact_gelu, hidden)
    activated = activated_float.astype(jnp.bfloat16)
    ffn_branch = branch_total(matmul(activated, contract_weight)) + contract_bias
    final_norm, third_back = jax.vjp(normalize, second_norm + ffn_branch, third_gain, third_shift)
    layer_output = final_norm.astype(jnp.bfloat16)
    grad_third_sum, grad_third_gain, grad_third_shift = third_back(output_grad.astype(jnp.float32))
    grad_ffn = grad_third_sum.astype(jnp.bfloat16)
    grad_contract_weight = contract_rows(activated, grad_ffn)
    grad_contract_bias = column_sums(grad_ffn)
    grad_hidden = gelu_back(times_transpose(grad_ffn, contract_weight))[0].astype(jnp.bfloat16)
    grad_expand_weight = contract_rows(second_low, grad_hidden)
    grad_expand_bias = column_sums(grad_hidden)
    ffn_summed = (grad_expand_weight, grad_contract_weight)
    grad_second = grad_third_sum + input_total(times_transpose(grad_hidden, expand_weight))
    grad_second_sum, grad_second_gain, grad_second_shift = second_back(grad_second)
    grad_cross = grad_second_sum.astype(jnp.bfloat16)
    grad_cross_output = contract_rows(cross_mixed, grad_cross)
    grad_cross_output_bias = column_sums(grad_cross)
    grad_cross_mixed = times_transpose(grad_cross, cross_output).astype(jnp.bfloat16)
    cross_grads = lax.map(
        partial(attend_back, False),
        (
            to_heads(cross_queries),
            to_heads(cross_keys),
            to_heads(cross_values),
            target_segments,
            memory_segments,
            cross_sums,
            to_heads(grad_cross_mixed),
        ),
    )
    grad_cross_queries = to_tokens(cross_grads[0])
    grad_cross_keys = to_tokens(cross_grads[1])
    grad_cross_values = to_tokens(cross_grads[2])
    grad_cross_query = contract_rows(first_low, grad_cross_queries)
    grad_cross_query_bias = column_sums(grad_cross_queries)
    grad_cross_key = contract_rows(memory, grad_cross_keys)
    grad_cross_value = contract_rows(memory, grad_cross_values)
    grad_cross_value_bias = column_sums(grad_cross_values)
    cross_summed = (grad_cross_query, grad_cross_key, grad_cross_value, grad_cross_output)
    memory_share = edge_total(
        times_transpose(grad_cross_keys, cross_key)
        + times_transpose(grad_cross_values, cross_value)
    )
    memory_grad = memory_share.astype(jnp.bfloat16)
    grad_first = grad_second_sum + input_total(times_transpose(grad_cross_queries, cross_query))
    grad_first_sum, grad_first_gain, grad_first_shift = first_back(grad_first)
    grad_self = grad_first_sum.astype(jnp.bfloat16)
    grad_self_output = contract_rows(self_mixed, grad_self)
    grad_self_output_bias = column_sums(grad_self)
    grad_self_mixed = times_transpose(grad_self, self_output).astype(jnp.bfloat16)
    self_grads = lax.map(
        partial(attend_back, True),
        (
            to_heads(self_queries),
            to_heads(self_keys),
            to_heads(self_values),
            target_segments,
            target_segments,
            self_sums,
            to_heads(grad_self_mixed),
        ),
    )
    grad_self_queries = to_tokens(self_grads[0])
    grad_self_keys = to_tokens(self_grads[1])
    grad_self_values = to_tokens(self_grads[2])
    grad_self_query = contract_rows(target, grad_self_queries)
    grad_self_query_bias = column_sums(grad_self_queries)
    grad_self_key = contract_rows(target, grad_self_keys)
    grad_self_value = contract_rows(target, grad_self_values)
    grad_self_value_bias = column_sums(grad_self_values)
    self_summed = (grad_self_query, grad_self_key, grad_self_value, grad_self_output)
    target_term = (
        times_transpose(grad_self_queries, self_query)
        + times_transpose(grad_self_keys, self_key)
        + times_transpose(grad_self_values, self_value)
    )
    target_share = edge_total(target_term)
    share_width = target_share.shape[1]
    residual_part = lax.dynamic_slice_in_dim(
        grad_first_sum, lax.axis_index("tensor") * share_width, share_width, 1
    )
    target_grad = (target_share + residual_part).astype(jnp.bfloat16)
    summed = (
        lax.psum_scatter(self_summed[0], "dp", scatter_dimension=0, tiled=True),
        lax.psum_scatter(self_summed[1], "dp", scatter_dimension=0, tiled=True),
        lax.psum_scatter(self_summed[2], "dp", scatter_dimension=0, tiled=True),
        lax.psum_scatter(self_summed[3], "dp", scatter_dimension=1, tiled=True),
        lax.psum_scatter(cross_summed[0], "dp", scatter_dimension=0, tiled=True),
        lax.psum_scatter(cross_summed[1], "dp", scatter_dimension=0, tiled=True),
        lax.psum_scatter(cross_summed[2], "dp", scatter_dimension=0, tiled=True),
        lax.psum_scatter(cross_summed[3], "dp", scatter_dimension=1, tiled=True),
        lax.psum_scatter(ffn_summed[0], "dp", scatter_dimension=0, tiled=True),
        lax.psum_scatter(ffn_summed[1], "dp", scatter_dimension=1, tiled=True),
    )
    vectors = lax.psum(
        (
            grad_self_query_bias,
            grad_self_value_bias,
            grad_self_output_bias,
            grad_first_gain,
            grad_first_shift,
            grad_cross_query_bias,
            grad_cross_value_bias,
            grad_cross_output_bias,
            grad_second_gain,
            grad_second_shift,
            grad_expand_bias,
            grad_contract_bias,
            grad_third_gain,
            grad_third_shift,
        ),
        "dp",
    )
    return (
        layer_output,
        target_grad,
        memory_grad,
        summed[0],
        vectors[0],
        summed[1],
        summed[2],
        vectors[1],
        summed[3],
        vectors[2],
        vectors[3],
        vectors[4],
        summed[4],
        vectors[5],
        summed[5],
        summed[6],
        vectors[6],
        summed[7],
        vectors[7],
        vectors[8],
        vectors[9],
        summed[8],
        vectors[10],
        summed[9],
        vectors[11],
        vectors[12],
        vectors[13],
    )


def solution(mesh):
    in_specs = (
        P("dp", None),
        P("dp", None),
        P("dp", None),
        P("dp", None),
        P(None, "tensor"),
        P("tensor"),
        P(None, "tensor"),
        P(None, "tensor"),
        P("tensor"),
        P("tensor", None),
        P(),
        P(),
        P(),
        P(None, "tensor"),
        P("tensor"),
        P(None, "tensor"),
        P(None, "tensor"),
        P("tensor"),
        P("tensor", None),
        P(),
        P(),
        P(),
        P(None, "tensor"),
        P("tensor"),
        P("tensor", None),
        P(),
        P(),
        P(),
        P("dp", None),
    )
    out_specs = (
        P("dp", None),
        P("dp", "tensor"),
        P("dp", "tensor"),
        P("dp", "tensor"),
        P("tensor"),
        P("dp", "tensor"),
        P("dp", "tensor"),
        P("tensor"),
        P("tensor", "dp"),
        P(),
        P(),
        P(),
        P("dp", "tensor"),
        P("tensor"),
        P("dp", "tensor"),
        P("dp", "tensor"),
        P("tensor"),
        P("tensor", "dp"),
        P(),
        P(),
        P(),
        P("dp", "tensor"),
        P("tensor"),
        P("tensor", "dp"),
        P(),
        P(),
        P(),
    )
    return jax.shard_map(
        per_device, mesh=mesh, in_specs=in_specs, out_specs=out_specs, check_vma=False
    )
```

profile of v0, /device:TPU:0, one launch (start us, length us, event | category | flops | bytes accessed | tf_op | source)
XLA Modules:
  0.0 1282.4 jit_solution(13164069724947715396)
XLA Ops:
  7.3 2.2 convolution_convert_fusion.3
  9.6 2.9 fusion.90
  15.3 19.3 %while.96 = (s32[]{:T(128)}, bf16[2,512,3,64]{1,3,2,0:T(8,128)(2,1)}, f32[2,3,512]{2,1,0:T(4,128)}, s32[2]{0:T(128)S(1)}, s32[1024]{0:T(1024)S(1)}, /*index=5*/b...) while((s32[]{:T(128)}, ...), condition=%wide.region_3.4_spmd, body=%wide.region_0.3_spmd.sunk | while | flops 423197696 | bytes 27042136 | solution.py:78
  17.2 2.3 fusion.230
  21.4 2.2 fusion.232
  26.9 2.3 fusion.230
  31.1 2.2 fusion.232
  37.0 3.3 fusion.109
  42.3 2.4 fusion.93
  44.6 119.6 %all-reduce.7.cloned.1.call-done = f32[1024,768]{1,0:T(8,128)} async-done(((f32[1024,768]{1,0:T(8,128)}), f32[1024,768]{1,0:T(8,128)}) %all-reduce.7.cloned.1.call-update) | async-done | bytes 3145744 | tf_op jit(solution)/shard_map/psum | solution.py:172
  164.3 2.4 fusion.105
  170.4 14.2 %while.97 = (s32[]{:T(128)}, bf16[2,512,3,64]{1,3,2,0:T(8,128)(2,1)S(1)}, f32[2,3,512]{2,1,0:T(4,128)S(1)}, s32[2]{0:T(128)S(1)}, s32[1024]{0:T(1024)S(1)}, /*in...) while((s32[]{:T(128)}, ...), condition=%wide.region_10.11_spmd, body=%wide.region_7.10_spmd.sunk | while | flops 422148608 | bytes 22221008 | solution.py:78
  175.2 2.2 fusion.237
  182.4 2.2 fusion.237
  186.4 3.4 fusion.110
  190.3 119.8 %all-reduce.9.cloned.1.call-done = f32[1024,768]{1,0:T(8,128)} async-done(((f32[1024,768]{1,0:T(8,128)}), f32[1024,768]{1,0:T(8,128)}) %all-reduce.9.cloned.1.call-update) | async-done | bytes 3145744 | tf_op jit(solution)/shard_map/psum | solution.py:172
  310.1 3.9 fusion.104
  316.2 9.8 multiply_convert_fusion.2
  327.2 3.1 fusion.111
  330.3 120.2 %all-reduce.11.cloned.1.call-done = f32[1024,768]{1,0:T(8,128)} async-done(((f32[1024,768]{1,0:T(8,128)}), f32[1024,768]{1,0:T(8,128)}) %all-reduce.11.cloned.1.call-update) | async-done | bytes 3145744 | tf_op jit(solution)/shard_map/psum | solution.py:172
  450.5 3.8 fusion.102
  457.7 2.6 fusion.101
  463.6 2.8 convert_reduce_fusion.2
  467.6 3.1 fusion.112
  471.0 120.0 %all-reduce.13.cloned.1.call-done = f32[1024,768]{1,0:T(8,128)} async-done(((f32[1024,768]{1,0:T(8,128)}), f32[1024,768]{1,0:T(8,128)}) %all-reduce.13.cloned.1.call-update) | async-done | bytes 3145744 | tf_op jit(solution)/shard_map/psum | solution.py:175
  591.0 5.4 multiply_reduce_fusion.2
  601.3 23.7 %while.98 = (s32[]{:T(128)}, f32[1024,3,64]{0,2,1:T(8,128)S(1)}, f32[1024,3,64]{0,2,1:T(8,128)}, bf16[2,512,3,64]{1,3,2,0:T(8,128)(2,1)}, s32[2]{0:T(128)S(1)}, ...) while((s32[]{:T(128)}, f32[1024,3,64]{0,2,1:T(8,128)S(1)}, ...), condition=%wide.region_24.25_spmd.clone, body=%wide.region_22.24_spmd.clone.sunk | while | flops 1031928320 | bytes 65659268 | solution.py:118
  606.9 2.5 multiply_reduce_fusion.11
  616.9 2.0 fusion.249
  618.8 2.5 multiply_reduce_fusion.11
  626.5 3.4 fusion.113
  630.8 3.2 convolution_bitcast_fusion
  634.3 115.9 %all-reduce.15.cloned.1.call-done = f32[1024,768]{1,0:T(8,128)} async-done(((f32[1024,768]{1,0:T(8,128)}), f32[1024,768]{1,0:T(8,128)}) %all-reduce.15.cloned.1.call-update) | async-done | bytes 3145744 | tf_op jit(solution)/shard_map/psum | solution.py:175
  750.2 5.4 multiply_reduce_fusion.3
  763.9 3.3 convolution_add_fusion
  767.3 3.4 convolution_convert_fusion
  771.5 24.3 %while.99 = (s32[]{:T(128)}, f32[1024,3,64]{0,2,1:T(8,128)S(1)}, f32[1024,3,64]{0,2,1:T(8,128)}, bf16[2,512,3,64]{1,3,2,0:T(8,128)(2,1)}, s32[2]{0:T(128)S(1)}, ...) while((s32[]{:T(128)}, f32[1024,3,64]{0,2,1:T(8,128)S(1)}, ...), condition=%wide.region_30.31_spmd.clone, body=%wide.region_28.30_spmd.clone.sunk | while | flops 1032977408 | bytes 65663364 | solution.py:118
  775.4 2.0 fusion.263
  777.4 2.5 multiply_reduce_fusion.12
  787.6 2.0 fusion.263
  789.5 2.5 multiply_reduce_fusion.12
  799.5 2.3 add_bitcast_fusion
  803.3 4.2 fusion.118
  807.7 5.6 fusion.106
  813.4 2.5 fusion.117
  815.9 2.3 convolution_bitcast_fusion.2
  818.2 2.4 copy.101
  820.7 2.3 convolution_bitcast_fusion.3
  823.0 2.2 copy.99
  826.6 2.3 copy.95
  829.0 2.3 convolution_bitcast_fusion.6
  831.3 2.2 copy.91
  835.0 2.3 copy.93
  842.3 25.8 %all-reduce = (f32[192]{0:T(256)}, f32[192]{0:T(256)}, f32[768]{0:T(1024)}, f32[768]{0:T(1024)}, f32[768]{0:T(1024)}, /*index=5*/f32[192]{0:T(256)}, f32[192]{0:...) all-reduce(f32[192]{0:T(256)S(1)} %reduce_sum.341, ...), channel_id=1, replica_groups=mesh['dp'=8,'tensor'=4] {'dp'}, use_global_device_ids=true, to_apply=%region_35.36 | all-reduce | flops 8448 | bytes 67584 | tf_op jit(solution)/shard_map/psum | solution.py:314
  869.7 18.2 %reduce-scatter.29.cloned.1.call-done = f32[1024,192]{0,1:T(8,128)} async-done(((f32[1024,768]{0,1:T(8,128)}), f32[1024,192]{0,1:T(8,128)}) %reduce-scatter.29.cloned.1.call-update) | async-done | bytes 786448 | tf_op jit(solution)/shard_map/reduce_scatter | solution.py:178
  889.9 60.7 %reduce-scatter.37.cloned.1.call-done = f32[192,1024]{1,0:T(8,128)} async-done(((f32[768,1024]{1,0:T(8,128)}), f32[192,1024]{1,0:T(8,128)}) %reduce-scatter.37.cloned.1.call-update) | async-done | bytes 786448
  954.8 42.2 %reduce-scatter.35.cloned.1.call-done = f32[768,96]{0,1:T(8,128)} async-done(((f32[768,768]{0,1:T(8,128)}), f32[768,96]{0,1:T(8,128)}) %reduce-scatter.35.cloned.1.call-update) | async-done | bytes 294928 | tf_op jit(solution)/shard_map/reduce_scatter | solution.py:312
  996.9 46.8 %reduce-scatter.33.cloned.1.call-done = f32[96,768]{1,0:T(8,128)} async-done(((f32[768,768]{1,0:T(8,128)}), f32[96,768]{1,0:T(8,128)}) %reduce-scatter.33.cloned.1.call-update) | async-done | bytes 294928 | tf_op jit(solution)/shard_map/reduce_scatter | solution.py:311
  1043.7 38.6 %reduce-scatter.31.cloned.1.call-done = f32[96,192]{1,0:T(8,128)} async-done(((f32[768,192]{1,0:T(8,128)}), f32[96,192]{1,0:T(8,128)}) %reduce-scatter.31.cloned.1.call-update) | async-done | bytes 73744 | tf_op jit(solution)/shard_map/reduce_scatter | solution.py:307
  1082.3 38.7 %reduce-scatter.49.cloned.1.call-done = f32[96,192]{1,0:T(8,128)} async-done(((f32[768,192]{1,0:T(8,128)}), f32[96,192]{1,0:T(8,128)}) %reduce-scatter.49.cloned.1.call-update) | async-done | bytes 73744
  1121.1 38.6 %reduce-scatter.47.cloned.1.call-done = f32[96,192]{1,0:T(8,128)} async-done(((f32[768,192]{1,0:T(8,128)}), f32[96,192]{1,0:T(8,128)}) %reduce-scatter.47.cloned.1.call-update) | async-done | bytes 73744
  1159.7 38.6 %reduce-scatter.43.cloned.1.call-done = f32[96,192]{1,0:T(8,128)} async-done(((f32[768,192]{1,0:T(8,128)}), f32[96,192]{1,0:T(8,128)}) %reduce-scatter.43.cloned.1.call-update) | async-done | bytes 73744
  1198.3 38.6 %reduce-scatter.39.cloned.1.call-done = f32[96,192]{1,0:T(8,128)} async-done(((f32[768,192]{1,0:T(8,128)}), f32[96,192]{1,0:T(8,128)}) %reduce-scatter.39.cloned.1.call-update) | async-done | bytes 73744
  1236.9 38.6 %reduce-scatter.41.cloned.1.call-done = f32[96,192]{1,0:T(8,128)} async-done(((f32[768,192]{1,0:T(8,128)}), f32[96,192]{1,0:T(8,128)}) %reduce-scatter.41.cloned.1.call-update) | async-done | bytes 73744
  (411 shorter events, 108.1 us)
Async XLA Ops:
  7.2 33.4 %copy-start = (bf16[1024,768]{1,0:T(8,128)(2,1)S(1)}, bf16[1024,768]{1,0:T(8,128)(2,1)}, u32[]{:S(2)}) copy-start(bf16[1024,768]{1,0:T(8,128)(2,1)} %param.38) | copy-start | bytes 4718596
  7.2 5.3 copy-start.10
  7.2 5.3 copy-start.101
  7.2 157.0 %all-reduce.7.cloned.1.call-start = ((), (), s32[]{:S(2)}) async-start(), calls=%async_computation.12 | async-start | bytes 6291456 | tf_op jit(solution)/shard_map/psum | solution.py:172
  7.3 5.2 copy-start.46
  9.5 5.8 copy-start.35
  34.6 5.7 copy-start.3
  40.3 123.9 %copy-start.89 = (f32[768]{0:T(1024)S(1)}, f32[768]{0:T(1024)}, u32[]{:S(2)}) copy-start(f32[768]{0:T(1024)} %param.47) | copy-start | bytes 9220
  40.3 269.7 %all-reduce.9.cloned.1.call-start = ((), (), s32[]{:S(2)}) async-start(), calls=%async_computation.13 | async-start | bytes 6291456 | tf_op jit(solution)/shard_map/psum | solution.py:172
  168.2 141.9 %copy-start.58 = (f32[1024]{0:T(1024)}, f32[1024]{0:T(1024)S(1)}, u32[]{:S(2)}) copy-start(f32[1024]{0:T(1024)S(1)} %fusion.94) | copy-start | bytes 12292
  186.4 123.6 %copy-start.61 = (f32[768]{0:T(1024)S(1)}, f32[768]{0:T(1024)}, u32[]{:S(2)}) copy-start(f32[768]{0:T(1024)} %param.48) | copy-start | bytes 9220
  186.4 123.6 %copy-start.81 = (f32[768]{0:T(1024)S(1)}, f32[768]{0:T(1024)}, u32[]{:S(2)}) copy-start(f32[768]{0:T(1024)} %param.49) | copy-start | bytes 9220
  186.4 123.6 %copy-start.90 = (f32[768]{0:T(1024)S(1)}, f32[768]{0:T(1024)}, u32[]{:S(2)}) copy-start(f32[768]{0:T(1024)} %param.56) | copy-start | bytes 9220
  189.8 260.7 %all-reduce.11.cloned.1.call-start = ((), (), s32[]{:S(2)}) async-start(), calls=%async_computation.14 | async-start | bytes 6291456 | tf_op jit(solution)/shard_map/psum | solution.py:172
  313.9 12.0 copy-start.5
  314.0 282.4 %copy-start.56 = (f32[1024]{0:T(1024)}, f32[1024]{0:T(1024)S(1)}, u32[]{:S(2)}) copy-start(f32[1024]{0:T(1024)S(1)} %broadcast_multiply_fusion.1) | copy-start | bytes 12292
  314.5 11.4 copy-start.74
  316.2 134.3 %copy-start.63 = (f32[1024]{0:T(1024)}, f32[1024]{0:T(1024)S(1)}, u32[]{:S(2)}) copy-start(f32[1024]{0:T(1024)S(1)} %fusion.95) | copy-start | bytes 12292
  316.2 11.0 copy-start.96
  330.2 120.3 %copy-start.91 = (f32[768]{0:T(1024)S(1)}, f32[768]{0:T(1024)}, u32[]{:S(2)}) copy-start(f32[768]{0:T(1024)} %param.62) | copy-start | bytes 9220
  330.3 260.7 %all-reduce.13.cloned.1.call-start = ((), (), s32[]{:S(2)}) async-start(), calls=%async_computation.15 | async-start | bytes 6291456 | tf_op jit(solution)/shard_map/psum | solution.py:175
  457.6 5.2 copy-start.107
  470.7 279.5 %all-reduce.15.cloned.1.call-start = ((), (), s32[]{:S(2)}) async-start(), calls=%async_computation.16 | async-start | bytes 6291456 | tf_op jit(solution)/shard_map/psum | solution.py:175
  591.0 5.4 copy-start.75
  591.0 5.5 copy-start.6
  591.0 5.5 copy-start.64
  591.0 5.5 copy-start.67
  629.9 120.2 %copy-start.59 = (f32[1024]{0:T(1024)S(1)}, f32[1024]{0:T(1024)}, u32[]{:S(2)}) copy-start(f32[1024]{0:T(1024)} %copy-done.58) | copy-start | bytes 12292
  629.9 120.2 %copy-start.62 = (f32[768]{0:T(1024)S(1)}, f32[768]{0:T(1024)}, u32[]{:S(2)}) copy-start(f32[768]{0:T(1024)} %param.48) | copy-start | bytes 9220
  630.0 209.3 %reduce-scatter.51.cloned.1.call-start = ((), (), s32[]{:S(2)}) async-start(), calls=%async_computation.28 | async-start | bytes 884736
  630.0 120.2 %copy-start.70 = (f32[1024]{0:T(1024)S(1)}, f32[1024]{0:T(1024)}, u32[]{:S(2)}) copy-start(f32[1024]{0:T(1024)} %copy-done.69) | copy-start | bytes 12292
  634.0 121.5 %copy-start.73 = (f32[1024]{0:T(1024)S(1)}, f32[1024]{0:T(1024)}, u32[]{:S(2)}) copy-start(f32[1024]{0:T(1024)} %copy-done.72) | copy-start | bytes 12292
  634.0 234.1 %reduce-scatter.45.cloned.1.call-start = ((), (), s32[]{:S(2)}) async-start(), calls=%async_computation.25 | async-start | bytes 884736
  750.2 5.4 copy-start.2
  761.3 126.6 %reduce-scatter.29.cloned.1.call-start = ((), (), s32[]{:S(2)}) async-start(), calls=%async_computation.17 | async-start | bytes 3932160 | tf_op jit(solution)/shard_map/reduce_scatter | solution.py:178
  767.2 4.3 copy-start.12
  767.2 4.3 copy-start.14
  767.3 183.3 %reduce-scatter.37.cloned.1.call-start = ((), (), s32[]{:S(2)}) async-start(), calls=%async_computation.21 | async-start | bytes 3932160
  801.9 5.7 copy-start.57
  801.9 5.7 copy-start.65
  801.9 5.7 copy-start.68
  801.9 5.7 copy-start.94
  802.0 195.0 %reduce-scatter.35.cloned.1.call-start = ((), (), s32[]{:S(2)}) async-start(), calls=%async_computation.20 | async-start | bytes 2654208 | tf_op jit(solution)/shard_map/reduce_scatter | solution.py:312
  807.6 5.8 copy-start.17
  807.6 236.2 %reduce-scatter.33.cloned.1.call-start = ((), (), s32[]{:S(2)}) async-start(), calls=%async_computation.19 | async-start | bytes 2654208 | tf_op jit(solution)/shard_map/reduce_scatter | solution.py:311
  813.3 269.0 %reduce-scatter.31.cloned.1.call-start = ((), (), s32[]{:S(2)}) async-start(), calls=%async_computation.18 | async-start | bytes 884736 | tf_op jit(solution)/shard_map/reduce_scatter | solution.py:307
  815.9 305.2 %reduce-scatter.49.cloned.1.call-start = ((), (), s32[]{:S(2)}) async-start(), calls=%async_computation.27 | async-start | bytes 884736
  818.2 7.1 copy-start.11
  820.6 339.0 %reduce-scatter.47.cloned.1.call-start = ((), (), s32[]{:S(2)}) async-start(), calls=%async_computation.26 | async-start | bytes 884736
  825.3 373.0 %reduce-scatter.43.cloned.1.call-start = ((), (), s32[]{:S(2)}) async-start(), calls=%async_computation.24 | async-start | bytes 884736
  826.6 7.0 copy-start.26
  828.9 407.9 %reduce-scatter.39.cloned.1.call-start = ((), (), s32[]{:S(2)}) async-start(), calls=%async_computation.22 | async-start | bytes 884736
  833.5 8.7 copy-start.76
  833.5 8.7 copy-start.77
  833.5 8.7 copy-start.78
  833.5 8.7 copy-start.79
  833.5 441.9 %reduce-scatter.41.cloned.1.call-start = ((), (), s32[]{:S(2)}) async-start(), calls=%async_computation.23 | async-start | bytes 884736
  834.9 7.2 copy-start.88
  834.9 7.3 copy-start.83
  834.9 7.3 copy-start.84
  834.9 7.3 copy-start.85
  834.9 7.3 copy-start.86
  834.9 7.3 copy-start.87
  835.0 7.3 copy-start.95
  (76 other events, 139.5 us)
Sparse Core Ops, SparseCore 0:
  40.4 123.7 all-reduce.6
  189.9 120.0 all-reduce.8
  330.4 120.0 all-reduce.10
  470.8 120.0 all-reduce.12
  630.0 120.0 all-reduce.14
  753.2 33.9 reduce-scatter.50
  790.3 34.9 reduce-scatter.44
  827.7 60.2 reduce-scatter.28
  890.3 60.2 reduce-scatter.36
  954.4 42.5 reduce-scatter.34
  1001.2 42.4 reduce-scatter.32
  1047.3 34.9 reduce-scatter.30
  1086.0 34.9 reduce-scatter.48
  1124.6 34.9 reduce-scatter.46
  1163.2 34.9 reduce-scatter.42
  1201.8 34.9 reduce-scatter.38
  1240.4 34.9 reduce-scatter.40
where the time goes:
time: 1290 us; the launch traced here: 1280 us
  waiting for transfers between devices  995 us (77%)
  matrix products  125 us (10%)
  other arithmetic  60.8 us (5%)
  local copies, waits for them, and re-layouts  52.4 us (4%)
  blocking collectives  25.8 us (2%)
  between operations  15.5 us (1%)
    psum x3, waiting for transfers between devices, branch_total(): return lax.psum(partial_term, 'tensor')  360 us
    unnamed x25, waiting for transfers between devices  254 us
    psum x2, waiting for transfers between devices, input_total(): return lax.psum(partial_term, 'tensor')  236 us
    reduce_scatter x1, waiting for transfers between devices, per_device(): lax.psum_scatter(ffn_summed[0], 'dp', scatter_dimension=0, tiled=True)  46.8 us
    reduce_scatter x1, waiting for transfers between devices, per_device(): lax.psum_scatter(ffn_summed[1], 'dp', scatter_dimension=1, tiled=True)  42.2 us
    reduce_scatter x1, waiting for transfers between devices, per_device(): lax.psum_scatter(cross_summed[0], 'dp', scatter_dimension=0, tiled=True)  38.6 us
    unnamed x199, local copies, waits for them, and re-layouts  31.8 us
    dot_general x10, matrix products, matmul(): return jnp.dot(left_side, right_side, preferred_element_type=jnp.float32)  30.7 us
  transfers between devices with their start and end apart: 17, of which 15 were waited for; matrix products, arithmetic and copies ran while one was open for 8% of the time, Pallas kernels for 0%

commit v1 on v0

v1 whole, which is shorter than its diff:
```python
from functools import partial

import jax
import jax.numpy as jnp
from jax import lax
from jax.experimental import pallas as pl
from jax.experimental.pallas import tpu as pltpu
from jax.sharding import PartitionSpec as P

HEAD_DIM = 64
EPSILON = 1e-05
NEGATIVE = -1e30
BF = jnp.bfloat16
F32 = jnp.float32
MESH = pl.DeviceIdType.MESH
MIB = 2**20


def dot_nn(a, b):
    return lax.dot_general(a, b, (((1,), (0,)), ((), ())), preferred_element_type=F32)


def dot_nt(a, b):
    return lax.dot_general(a, b, (((1,), (1,)), ((), ())), preferred_element_type=F32)


def dot_tn(a, b):
    return lax.dot_general(a, b, (((0,), (0,)), ((), ())), preferred_element_type=F32)


def normalize(summed, norm_gain, norm_shift):
    center = jnp.mean(summed, axis=-1, keepdims=True)
    centered = summed - center
    spread = jnp.mean(centered * centered, axis=-1, keepdims=True)
    return centered * lax.rsqrt(spread + EPSILON) * norm_gain + norm_shift


def exact_gelu(values):
    return jax.nn.gelu(values, approximate=False)


def column_sums(values):
    return jnp.sum(values.astype(F32), axis=0)


def row_groups(width, hidden):
    half = 2 * width
    sizes = [half, half, half, half, hidden, hidden]
    starts = [sum(sizes[:i]) for i in range(len(sizes))]
    return list(zip(starts, sizes, strict=True))


def gather_kernel(
    groups, n_dp, n_tensor, chunk_ref, bias_ref, own_ref, found_ref, full_ref, bias_out_ref, stage, low, send_sem, recv_sem,
    bias_send, bias_recv, local_sem
):
    d = lax.axis_index("dp")
    z = lax.axis_index("tensor")
    bit_c = d % 2
    bit_x = (d // 2) % 2
    bit_y = d // 4
    dc = d + 1 - 2 * bit_c
    dx = d + 2 - 4 * bit_x
    dy = d + 4 - 8 * bit_y
    dxy = dx + 4 - 8 * bit_y
    barrier = pltpu.get_barrier_semaphore()
    for k in range(1, n_tensor):
        pl.semaphore_signal(barrier, inc=1, device_id={"tensor": (z + k) % n_tensor}, device_id_type=MESH)
    for other in (dc, dx, dy):
        pl.semaphore_signal(barrier, inc=1, device_id={"dp": other}, device_id_type=MESH)
    pl.semaphore_wait(barrier, n_tensor + 2)

    spans = []
    at = 0
    for _, size in groups:
        spans.append((at, size // n_dp))
        at += size // n_dp

    def to_z(g, k):
        start, rows = spans[g]
        return pltpu.make_async_remote_copy(
            src_ref=chunk_ref.at[pl.ds(start, rows)],
            dst_ref=found_ref.at[d, k, pl.ds(start, rows)],
            send_sem=send_sem.at[g, k],
            recv_sem=recv_sem.at[g, k],
            device_id={"tensor": (z + k + 1) % n_tensor},
            device_id_type=MESH,
        )

    def in_plane(g, slot, chunk, first, rows, other):
        piece = found_ref.at[chunk, :, pl.ds(first, rows)]
        return pltpu.make_async_remote_copy(
            src_ref=piece,
            dst_ref=piece,
            send_sem=send_sem.at[g, slot],
            recv_sem=recv_sem.at[g, slot],
            device_id={"dp": other},
            device_id_type=MESH,
        )

    def bias_copy(k):
        return pltpu.make_async_remote_copy(
            src_ref=bias_ref,
            dst_ref=bias_out_ref.at[z],
            send_sem=bias_send.at[k],
            recv_sem=bias_recv.at[k],
            device_id={"tensor": (z + k + 1) % n_tensor},
            device_id_type=MESH,
        )

    def own_x(g):
        return in_plane(g, 3, d, *spans[g], dx)

    def own_y(g):
        return in_plane(g, 4, d, *spans[g], dy)

    def own_c(g):
        return in_plane(g, 5, d, *spans[g], dc)

    def pass_y(g):
        start, rows = spans[g]
        return in_plane(g, 6, dx, start, rows // 2, dy)

    def pass_x(g):
        start, rows = spans[g]
        return in_plane(g, 7, dy, start + rows // 2, rows // 2, dx)

    def pass_c(g, i):
        return in_plane(g, 8 + i, (dx, dy, dxy)[i], *spans[g], dc)

    def arrive(g, slot, chunk, first, rows):
        in_plane(g, slot, chunk, first, rows, dc).wait_recv()

    count = len(groups)
    for k in range(n_tensor - 1):
        bias_copy(k).start()
    own_bias = pltpu.make_async_copy(bias_ref, bias_out_ref.at[z], local_sem.at[4])
    own_bias.start()
    for g in range(count):
        for k in range(n_tensor - 1):
            to_z(g, k).start()

    def stage_in(g):
        for k in range(n_tensor - 1):
            to_z(g, k).wait_recv()
        own_x(g).start()
        own_y(g).start()
        own_c(g).start()

    def stage_pass(g):
        start, rows = spans[g]
        arrive(g, 3, dx, start, rows)
        pass_y(g).start()
        pass_c(g, 0).start()
        arrive(g, 4, dy, start, rows)
        pass_x(g).start()
        pass_c(g, 1).start()

    def stage_last(g):
        start, rows = spans[g]
        arrive(g, 6, dxy, start, rows // 2)
        arrive(g, 7, dxy, start + rows // 2, rows // 2)
        pass_c(g, 2).start()

    def stage_out(g):
        start, rows = spans[g]
        arrive(g, 5, dc, start, rows)
        for i in range(3):
            arrive(g, 8 + i, dc, start, rows)
        first, size = groups[g]
        for k in range(n_tensor):
            slot = k % 2
            s = (z + n_tensor - 1 - k) % n_tensor
            low_piece = low.at[slot, pl.ds(0, size)]
            if k < n_tensor - 1:
                piece = stage.at[:, pl.ds(0, rows)]
                load = pltpu.make_async_copy(found_ref.at[:, k, pl.ds(start, rows)], piece, local_sem.at[slot])
                load.start()
                load.wait()
                low[slot, pl.ds(0, size)] = stage[:, pl.ds(0, rows)].reshape(size, stage.shape[2]).astype(BF)
            else:
                load = pltpu.make_async_copy(own_ref.at[pl.ds(first, size)], low_piece, local_sem.at[slot])
                load.start()
                load.wait()
            store = pltpu.make_async_copy(low_piece, full_ref.at[s, pl.ds(first, size)], local_sem.at[2 + slot])
            store.start()
            store.wait()

    for g in range(count + 3):
        if g < count:
            stage_in(g)
        if 0 <= g - 1 < count:
            stage_pass(g - 1)
        if 0 <= g - 2 < count:
            stage_last(g - 2)
        if 0 <= g - 3 < count:
            stage_out(g - 3)
    own_bias.wait()
    for k in range(n_tensor - 1):
        bias_copy(k).wait_recv()
        bias_copy(k).wait_send()
    for g in range(count):
        for k in range(n_tensor - 1):
            to_z(g, k).wait_send()
        own_x(g).wait_send()
        own_y(g).wait_send()
        own_c(g).wait_send()
        pass_y(g).wait_send()
        pass_x(g).wait_send()
        for i in range(3):
            pass_c(g, i).wait_send()


def round_kernel(wide_ref, low_ref):
    low_ref[...] = wide_ref[...].astype(BF)


def rounded(array):
    slices, rows, width = array.shape
    block = pl.BlockSpec((1, rows // 4, width), lambda i, j: (i, j, 0))
    return pl.pallas_call(
        round_kernel,
        grid=(slices, 4),
        in_specs=[block],
        out_specs=block,
        out_shape=jax.ShapeDtypeStruct(array.shape, BF),
    )(array)


def gather_weights(own, biases, groups, n_dp, n_tensor):
    rows, width = own.shape
    if n_dp != 8 or n_tensor != 4:
        full = lax.all_gather(own.astype(F32), "tensor", axis=0)
        return rounded(full), lax.all_gather(biases, "tensor", axis=0)
    d = lax.axis_index("dp")
    pieces = [
        lax.dynamic_slice_in_dim(own, start + d * (size // n_dp), size // n_dp, 0) for start, size in groups
    ]
    chunk = jnp.concatenate(pieces, axis=0).astype(F32)
    most = max(size for _, size in groups)
    anywhere = pl.BlockSpec(memory_space=pl.ANY)
    _, full, all_biases = pl.pallas_call(
        partial(gather_kernel, groups, n_dp, n_tensor),
        out_shape=(
            jax.ShapeDtypeStruct((n_dp, n_tensor - 1, rows // n_dp, width), F32),
            jax.ShapeDtypeStruct((n_tensor, rows, width), BF),
            jax.ShapeDtypeStruct((n_tensor,) + biases.shape, F32),
        ),
        in_specs=[anywhere] * 3,
        out_specs=[anywhere] * 3,
        scratch_shapes=[
            pltpu.VMEM((n_dp, most // n_dp, width), F32),
            pltpu.VMEM((2, most, width), BF),
            pltpu.SemaphoreType.DMA((len(groups), 11)),
            pltpu.SemaphoreType.DMA((len(groups), 11)),
            pltpu.SemaphoreType.DMA((n_tensor - 1,)),
            pltpu.SemaphoreType.DMA((n_tensor - 1,)),
            pltpu.SemaphoreType.DMA((5,)),
        ],
        compiler_params=pltpu.CompilerParams(collective_id=0, has_side_effects=True, vmem_limit_bytes=32 * MIB),
    )(chunk, biases, own)
    return full, all_biases


def attend_kernel(block, causal, q_ref, k_ref, v_ref, q_ids_ref, k_ids_ref, mixed_ref, sums_ref):
    length = q_ref.shape[0]
    lane = lax.broadcasted_iota(jnp.int32, (1, 2 * HEAD_DIM), 1)
    k_ids = k_ids_ref[...]
    for start in range(0, length, block):
        reach = start + block if causal else length
        queries = q_ref[start : start + block, :] * jnp.asarray(HEAD_DIM**-0.5, BF)
        allowed = q_ids_ref[start : start + block, :] == k_ids[:, :reach]
        if causal:
            allowed = allowed & (
                lax.broadcasted_iota(jnp.int32, (block, reach), 0) + start
                >= lax.broadcasted_iota(jnp.int32, (block, reach), 1)
            )
        outs, logs = [], []
        for head in range(2):
            mine = (lane < HEAD_DIM) if head == 0 else (lane >= HEAD_DIM)
            scores = dot_nt(jnp.where(mine, queries, jnp.zeros_like(queries)), k_ref[:reach, :])
            scores = jnp.where(allowed, scores, NEGATIVE)
            top = jnp.max(scores, axis=1, keepdims=True)
            weights = jnp.exp(scores - top)
            total = jnp.sum(weights, axis=1, keepdims=True)
            outs.append(dot_nn(weights.astype(BF), v_ref[:reach, :]) * (1.0 / total))
            logs.append(top + jnp.log(total))
        mixed_ref[start : start + block, :] = jnp.where(lane < HEAD_DIM, outs[0], outs[1]).astype(BF)
        sums_ref[start : start + block, :] = jnp.where(lane < HEAD_DIM, logs[0], logs[1])


def attend(causal, queries, keys, values, query_ids, key_ids):
    length, width = queries.shape
    pair = 2 * HEAD_DIM
    wide = pl.BlockSpec((length, pair), lambda i: (0, i))
    return pl.pallas_call(
        partial(attend_kernel, 512, causal),
        grid=(width // pair,),
        in_specs=[wide] * 3 + [pl.BlockSpec((length, 1), lambda i: (0, 0)), pl.BlockSpec((1, length), lambda i: (0, 0))],
        out_specs=[wide] * 2,
        out_shape=[jax.ShapeDtypeStruct((length, width), BF), jax.ShapeDtypeStruct((length, width), F32)],
        compiler_params=pltpu.CompilerParams(vmem_limit_bytes=60 * MIB),
    )(queries, keys, values, query_ids.reshape(length, 1), key_ids.reshape(1, length))


def attend_back_kernel(
    block, causal, q_ref, k_ref, v_ref, gm_ref, mixed_ref, sums_ref, q_ids_ref, k_ids_ref, gq_ref, gk_ref, gv_ref, gq_sum,
    logs, dots
):
    length = q_ref.shape[0]
    lane = lax.broadcasted_iota(jnp.int32, (1, 2 * HEAD_DIM), 1)
    scale = HEAD_DIM**-0.5
    gq_sum[...] = jnp.zeros_like(gq_sum)
    logs[...] = jnp.transpose(sums_ref[...])
    products = jnp.transpose(gm_ref[...].astype(F32) * mixed_ref[...].astype(F32))
    dots[0:1, :] = jnp.sum(products[:HEAD_DIM], axis=0, keepdims=True)
    dots[1:2, :] = jnp.sum(products[HEAD_DIM:], axis=0, keepdims=True)
    for start in range(0, length, block):
        first = start if causal else 0
        reach = length - first
        keys = k_ref[start : start + block, :]
        values = v_ref[start : start + block, :]
        allowed = k_ids_ref[start : start + block, :] == q_ids_ref[:, first:]
        if causal:
            allowed = allowed & (
                lax.broadcasted_iota(jnp.int32, (block, reach), 0) + start
                <= lax.broadcasted_iota(jnp.int32, (block, reach), 1) + first
            )
        gk = jnp.zeros((block, 2 * HEAD_DIM), F32)
        gv = jnp.zeros((block, 2 * HEAD_DIM), F32)
        queries = q_ref[first:, :]
        gm = gm_ref[first:, :]
        for head in range(2):
            mine = (lane < HEAD_DIM) if head == 0 else (lane >= HEAD_DIM)
            keys_h = jnp.where(mine, keys, jnp.zeros_like(keys))
            values_h = jnp.where(mine, values, jnp.zeros_like(values))
            scores = dot_nt(keys_h * jnp.asarray(scale, BF), queries)
            probs = jnp.where(allowed, jnp.exp(scores - logs[HEAD_DIM * head : HEAD_DIM * head + 1, first:]), 0.0)
            grad_probs = dot_nt(values_h, gm)
            grad_scores = (probs * (grad_probs - dots[head : head + 1, first:])).astype(BF)
            gv = gv + dot_nn(probs.astype(BF), jnp.where(mine, gm, jnp.zeros_like(gm)))
            gk = gk + dot_nn(grad_scores, jnp.where(mine, queries, jnp.zeros_like(queries)))
            gq_sum[first:, :] += dot_tn(grad_scores, keys_h)
        gk_ref[start : start + block, :] = (gk * scale).astype(BF)
        gv_ref[start : start + block, :] = gv.astype(BF)
    gq_ref[...] = (gq_sum[...] * scale).astype(BF)


def attend_back(causal, queries, keys, values, grad_mixed, mixed, sums, query_ids, key_ids):
    length, width = queries.shape
    pair = 2 * HEAD_DIM
    wide = pl.BlockSpec((length, pair), lambda i: (0, i))
    low = jax.ShapeDtypeStruct((length, width), BF)
    return pl.pallas_call(
        partial(attend_back_kernel, 256, causal),
        grid=(width // pair,),
        in_specs=[wide] * 6 + [pl.BlockSpec((1, length), lambda i: (0, 0)), pl.BlockSpec((length, 1), lambda i: (0, 0))],
        out_specs=[wide] * 3,
        out_shape=[low] * 3,
        scratch_shapes=[
            pltpu.VMEM((length, pair), F32),
            pltpu.VMEM((pair, length), F32),
            pltpu.VMEM((8, length), F32),
        ],
        compiler_params=pltpu.CompilerParams(vmem_limit_bytes=60 * MIB),
    )(queries, keys, values, grad_mixed, mixed, sums, query_ids.reshape(1, length), key_ids.reshape(length, 1))


def per_device(
    n_dp,
    n_tensor,
    target,
    memory,
    target_segments,
    memory_segments,
    self_query,
    self_query_bias,
    self_key,
    self_value,
    self_value_bias,
    self_output,
    self_output_bias,
    first_gain,
    first_shift,
    cross_query,
    cross_query_bias,
    cross_key,
    cross_value,
    cross_value_bias,
    cross_output,
    cross_output_bias,
    second_gain,
    second_shift,
    expand_weight,
    expand_bias,
    contract_weight,
    contract_bias,
    third_gain,
    third_shift,
    output_grad,
):
    model, width = self_query.shape
    hidden_own = expand_weight.shape[1]
    z = lax.axis_index("tensor")
    heads_all = width * n_tensor

    own = jnp.concatenate(
        (
            self_query.T,
            self_key.T,
            self_value.T,
            self_output,
            cross_key.T,
            cross_value.T,
            cross_query.T,
            cross_output,
            expand_weight.T,
            contract_weight,
        ),
        axis=0,
    )
    biases = jnp.concatenate((self_query_bias, self_value_bias, cross_query_bias, cross_value_bias, expand_bias))
    bias_count = biases.shape[0]
    bias_rows = -(-bias_count // 1024) * 8
    biases = jnp.pad(biases, (0, bias_rows * 128 - bias_count)).reshape(bias_rows, 128)
    groups = row_groups(width, hidden_own)
    full, all_biases = gather_weights(own, biases, groups, n_dp, n_tensor)

    def matrix(index):
        return full[:, index * width : (index + 1) * width].reshape(heads_all, model)

    w_sq, w_sk, w_sv, w_so, w_ck, w_cv, w_cq, w_co = (matrix(i) for i in range(8))
    w_ex = full[:, 8 * width : 8 * width + hidden_own].reshape(hidden_own * n_tensor, model)
    w_ct = full[:, 8 * width + hidden_own :].reshape(hidden_own * n_tensor, model)
    all_biases = all_biases.reshape(n_tensor, -1)
    b_sq, b_sv, b_cq, b_cv = (all_biases[:, i * width : (i + 1) * width].reshape(-1) for i in range(4))
    b_ex = all_biases[:, 4 * width : 4 * width + hidden_own].reshape(-1)

    target_ids = target_segments
    memory_ids = memory_segments

    self_queries = (dot_nt(target, w_sq) + b_sq).astype(BF)
    self_keys = dot_nt(target, w_sk).astype(BF)
    self_values = (dot_nt(target, w_sv) + b_sv).astype(BF)
    self_mixed, self_sums = attend(True, self_queries, self_keys, self_values, target_ids, target_ids)
    self_branch = dot_nn(self_mixed, w_so) + self_output_bias
    first_norm, first_back = jax.vjp(normalize, target.astype(F32) + self_branch, first_gain, first_shift)
    first_low = first_norm.astype(BF)
    cross_queries = (dot_nt(first_low, w_cq) + b_cq).astype(BF)
    cross_keys = dot_nt(memory, w_ck).astype(BF)
    cross_values = (dot_nt(memory, w_cv) + b_cv).astype(BF)
    cross_mixed, cross_sums = attend(False, cross_queries, cross_keys, cross_values, target_ids, memory_ids)
    cross_branch = dot_nn(cross_mixed, w_co) + cross_output_bias
    second_norm, second_back = jax.vjp(normalize, first_norm + cross_branch, second_gain, second_shift)
    second_low = second_norm.astype(BF)
    hidden = dot_nt(second_low, w_ex) + b_ex
    activated_float, gelu_back = jax.vjp(exact_gelu, hidden)
    activated = activated_float.astype(BF)
    ffn_branch = dot_nn(activated, w_ct) + contract_bias
    final_norm, third_back = jax.vjp(normalize, second_norm + ffn_branch, third_gain, third_shift)
    layer_output = final_norm.astype(BF)
    grad_third_sum, grad_third_gain, grad_third_shift = third_back(output_grad.astype(F32))
    grad_ffn = grad_third_sum.astype(BF)
    grad_hidden = gelu_back(dot_nt(grad_ffn, w_ct))[0].astype(BF)

    def own_hidden(array):
        return lax.dynamic_slice_in_dim(array, z * hidden_own, hidden_own, 1)

    def own_heads(array):
        return lax.dynamic_slice_in_dim(array, z * width, width, 1)

    grad_contract = dot_tn(grad_ffn, own_hidden(activated))
    grad_contract_bias = column_sums(grad_ffn)
    grad_hidden_own = own_hidden(grad_hidden)
    grad_expand = dot_tn(second_low, grad_hidden_own)
    grad_expand_bias = column_sums(grad_hidden_own)
    grad_second = grad_third_sum + dot_nn(grad_hidden, w_ex)
    grad_second_sum, grad_second_gain, grad_second_shift = second_back(grad_second)
    grad_cross = grad_second_sum.astype(BF)
    grad_cross_output = dot_tn(grad_cross, own_heads(cross_mixed))
    grad_cross_output_bias = column_sums(grad_cross)
    grad_cross_mixed = dot_nt(grad_cross, w_co).astype(BF)
    gcq, gck, gcv = attend_back(
        False, cross_queries, cross_keys, cross_values, grad_cross_mixed, cross_mixed, cross_sums, target_ids, memory_ids
    )
    gcq_own, gck_own, gcv_own = own_heads(gcq), own_heads(gck), own_heads(gcv)
    grad_cross_query = dot_tn(first_low, gcq_own)
    grad_cross_query_bias = column_sums(gcq_own)
    grad_cross_key = dot_tn(memory, gck_own)
    grad_cross_value = dot_tn(memory, gcv_own)
    grad_cross_value_bias = column_sums(gcv_own)
    share = model // n_tensor

    def columns(weight):
        return lax.dynamic_slice_in_dim(weight, z * share, share, 1)

    memory_grad = (dot_nn(gck, columns(w_ck)) + dot_nn(gcv, columns(w_cv))).astype(BF)
    grad_first = grad_second_sum + dot_nn(gcq, w_cq)
    grad_first_sum, grad_first_gain, grad_first_shift = first_back(grad_first)
    grad_self = grad_first_sum.astype(BF)
    grad_self_output = dot_tn(grad_self, own_heads(self_mixed))
    grad_self_output_bias = column_sums(grad_self)
    grad_self_mixed = dot_nt(grad_self, w_so).astype(BF)
    gsq, gsk, gsv = attend_back(
        True, self_queries, self_keys, self_values, grad_self_mixed, self_mixed, self_sums, target_ids, target_ids
    )
    gsq_own, gsk_own, gsv_own = own_heads(gsq), own_heads(gsk), own_heads(gsv)
    grad_self_query = dot_tn(target, gsq_own)
    grad_self_query_bias = column_sums(gsq_own)
    grad_self_key = dot_tn(target, gsk_own)
    grad_self_value = dot_tn(target, gsv_own)
    grad_self_value_bias = column_sums(gsv_own)
    target_grad = (
        lax.dynamic_slice_in_dim(grad_first_sum, z * share, share, 1)
        + dot_nn(gsq, columns(w_sq))
        + dot_nn(gsk, columns(w_sk))
        + dot_nn(gsv, columns(w_sv))
    ).astype(BF)

    partial_grads = jnp.concatenate(
        (
            grad_self_query,
            grad_self_key,
            grad_self_value,
            grad_self_output,
            grad_cross_query,
            grad_cross_key,
            grad_cross_value,
            grad_cross_output,
            grad_expand,
            grad_contract,
        ),
        axis=1,
    )
    total = lax.psum_scatter(partial_grads, "dp", scatter_dimension=0, tiled=True)
    parts = [total[:, i * width : (i + 1) * width] for i in range(8)]
    expand_total = total[:, 8 * width : 8 * width + hidden_own]
    contract_total = total[:, 8 * width + hidden_own :]
    vectors = (
        grad_self_query_bias,
        grad_self_value_bias,
        grad_self_output_bias,
        grad_first_gain,
        grad_first_shift,
        grad_cross_query_bias,
        grad_cross_value_bias,
        grad_cross_output_bias,
        grad_second_gain,
        grad_second_shift,
        grad_expand_bias,
        grad_contract_bias,
        grad_third_gain,
        grad_third_shift,
    )
    packed = lax.psum(jnp.concatenate(vectors), "dp")
    sums = []
    at = 0
    for vector in vectors:
        sums.append(packed[at : at + vector.shape[0]])
        at += vector.shape[0]
    return (
        layer_output,
        target_grad,
        memory_grad,
        parts[0],
        sums[0],
        parts[1],
        parts[2],
        sums[1],
        parts[3].T,
        sums[2],
        sums[3],
        sums[4],
        parts[4],
        sums[5],
        parts[5],
        parts[6],
        sums[6],
        parts[7].T,
        sums[7],
        sums[8],
        sums[9],
        expand_total,
        sums[10],
        contract_total.T,
        sums[11],
        sums[12],
        sums[13],
    )


def solution(mesh):
    rows = P("dp", None)
    split = P(None, "tensor")
    both = P("dp", "tensor")
    turned = P("tensor", "dp")
    own = P("tensor")
    in_specs = (
        rows, rows, rows, rows,
        split, own, split, split, own, P("tensor", None), P(), P(), P(),
        split, own, split, split, own, P("tensor", None), P(), P(), P(),
        split, own, P("tensor", None), P(), P(), P(),
        rows,
    )
    out_specs = (
        rows, both, both,
        both, own, both, both, own, turned, P(), P(), P(),
        both, own, both, both, own, turned, P(), P(), P(),
        both, own, turned, P(), P(), P(),
    )
    return jax.shard_map(
        partial(per_device, mesh.shape["dp"], mesh.shape["tensor"]),
        mesh=mesh,
        in_specs=in_specs,
        out_specs=out_specs,
        check_vma=False,
    )
```

time: 1290 us -> 626 us (0.49)
  waiting for transfers between devices: 995 us -> 33.9 us
  Pallas kernels: 0 us -> 300 us
  other arithmetic: 60.8 us -> 18.4 us
  matrix products: 125 us -> 156 us
  local copies, waits for them, and re-layouts: 52.4 us -> 69.9 us
    psum x5 -> x0, waiting for transfers between devices: 595 us -> none  [the longest x3 360 us: branch_total(): return lax.psum(partial_term, 'tensor')]
    pallas_call x0 -> x5, Pallas kernels: none -> 300 us  [the longest x1 179 us: gather_weights(): pl.pallas_call(partial(gather_kernel, groups, n_dp, n_tensor), out_shape=...]
    unnamed x25 -> x2, waiting for transfers between devices: 254 us -> 33.9 us
    reduce_scatter x4 -> x0, waiting for transfers between devices: 146 us -> none  [the longest x1 46.8 us: per_device(): lax.psum_scatter(ffn_summed[0], 'dp', scatter_dimension=0, tiled=True)]
    dot_general x56 -> x30, matrix products: 120 us -> 156 us  [the longest x10 80.3 us: dot_nt(): lax.dot_general(a, b, (((1,), (1,)), ((), ())), preferred_element_type=F32)]
    slice x0 -> x7, local copies, waits for them, and re-layouts: none -> 18.5 us  [the longest x1 8 us: per_device(): full[:, 8 * width + hidden_own:].reshape(hidden_own * n_tensor, model)]
    reduce_sum x14 -> x6, other arithmetic: 24.9 us -> 10.2 us  [column_sums(): return jnp.sum(values.astype(F32), axis=0)]
    unnamed x199 -> x150, local copies, waits for them, and re-layouts: 31.8 us -> 44.9 us
  transfers between devices with their start and end apart: 17 -> 1, of which waited for: 15 -> 1; matrix products, arithmetic and copies ran while one was open for 8% -> 3% of each run, Pallas kernels for 0% -> 0%
where the time goes in v1:
time: 626 us; the launch traced here: 616 us
  Pallas kernels  300 us (48%)
  matrix products  156 us (25%)
  local copies, waits for them, and re-layouts  69.9 us (11%)
  waiting for transfers between devices  33.9 us (5%)
  blocking collectives  23 us (4%)
  other arithmetic  18.4 us (3%)
  between operations  15.3 us (2%)
    pallas_call x1, Pallas kernels, gather_weights(): pl.pallas_call(partial(gather_kernel, groups, n_dp, n_tensor), out_shape=...  179 us
    dot_general x10, matrix products, dot_nt(): lax.dot_general(a, b, (((1,), (1,)), ((), ())), preferred_element_type=F32)  80.3 us
    pallas_call x2, Pallas kernels, attend_back(): pl.pallas_call(partial(attend_back_kernel, 256, causal), grid=(width // p...  74.4 us
    pallas_call x2, Pallas kernels, attend(): pl.pallas_call(partial(attend_kernel, 512, causal), grid=(width // pair,)...  46.6 us
    unnamed x150, local copies, waits for them, and re-layouts  44.9 us
    dot_general x10, matrix products, dot_nn(): lax.dot_general(a, b, (((1,), (0,)), ((), ())), preferred_element_type=F32)  43.7 us
    unnamed x2, waiting for transfers between devices  33.9 us
    dot_general x10, matrix products, dot_tn(): lax.dot_general(a, b, (((0,), (0,)), ((), ())), preferred_element_type=F32)  31.7 us
  transfers between devices with their start and end apart: 1, of which 1 were waited for; matrix products, arithmetic and copies ran while one was open for 3% of the time, Pallas kernels for 0%

profile of v1, /device:TPU:0, one launch (start us, length us, event | category | flops | bytes accessed | tf_op | source)
XLA Modules:
  0.0 615.9 jit_solution(16243366805390878779)
XLA Ops:
  7.3 1.8 bitcast_dynamic-update-slice_fusion.6
  9.1 1.6 copy.95
  12.2 1.7 constant_dynamic-update-slice_fusion.2
  13.9 1.7 bitcast_dynamic-update-slice_fusion.3
  15.6 1.7 bitcast_dynamic-update-slice_fusion.2
  26.6 2.3 copy-done.1
  29.0 178.7 %shard_map.484 = (f32[8,3,384,768]{3,2,1,0:T(8,128)}, bf16[4,3072,768]{2,1,0:T(8,128)(2,1)}, f32[4,16,128]{2,1,0:T(8,128)S(1)}) custom-call(f32[384,768]{1,0:T(8,128)S(1)} %convert_element_type.100.chunk_ref, f32[16,128]{1,0:T(8,128)S(1)} %pad_bitcast_fusion.bias_ref, bf16[3072,768]{1,0:T(8,128)(2,1)S(1)} %copy-done.1), custom_call_target="tpu_custom_call" | custom-call | tf_op jit(solution)/shard_map/pallas_call | solution.py:242
  207.6 7.0 %fusion.69 = (bf16[4,192,768]{2,1,0:T(8,128)(2,1)}, bf16[4,192,768]{2,1,0:T(8,128)(2,1)}, bf16[4,192,768]{2,1,0:T(8,128)(2,1)}, bf16[4,192,768]{2,1,0:T(8,128)(2...) fusion(bf16[4,3072,768]{2,1,0:T(8,128)(2,1)} %get-tuple-element.39), kind=kLoop, calls=%fused_computation.162 | loop fusion | bytes 18874368 | tf_op jit(solution)/shard_map/slice | solution.py:430
  214.6 8.0 %fusion.68 = (bf16[4,768,768]{2,1,0:T(8,128)(2,1)}, bf16[4,768,768]{2,1,0:T(8,128)(2,1)}) fusion(bf16[4,3072,768]{2,1,0:T(8,128)(2,1)} %get-tuple-element.39), kind=kLoop, calls=%fused_computation.161 | loop fusion | bytes 18874368 | tf_op jit(solution)/shard_map/slice | solution.py:434
  222.9 1.6 copy.94
  224.5 3.9 fusion.13.k_ref
  229.5 3.9 fusion.16.v_ref
  233.4 2.6 fusion.15.q_ref
  236.0 21.4 %shard_map.485 = (bf16[1024,768]{1,0:T(8,128)(2,1)}, f32[1024,768]{1,0:T(8,128)}) custom-call(bf16[1024,768]{1,0:T(8,128)(2,1)} %fusion.15.q_ref, bf16[1024,768]{1,0:T(8,128)(2,1)} %fusion.13.k_ref, bf16[1024,768]{1,0:T(8,128)(2,1)} %fusion.16.v_ref, s32[1024,1]{1,0:T(8,128)} %copy.99.q_ids_ref.k_ids_ref, s32[1,1024]{1,0:T(1,128)} %q_ids_ref.3), custom_call_target="tpu_custom_call" | custom-call | tf_op jit(solution)/shard_map/pallas_call | solution.py:296
  257.5 3.4 fusion.74
  260.9 1.7 copy-done.2
  263.1 2.6 fusion.14.k_ref
  265.7 2.6 fusion.17.v_ref
  268.9 1.2 copy-done.14
  270.0 2.6 add_convert_fusion.3.q_ref
  272.7 25.2 %shard_map.486 = (bf16[1024,768]{1,0:T(8,128)(2,1)}, f32[1024,768]{1,0:T(8,128)}) custom-call(bf16[1024,768]{1,0:T(8,128)(2,1)} %add_convert_fusion.3.q_ref, bf16[1024,768]{1,0:T(8,128)(2,1)} %fusion.14.k_ref, bf16[1024,768]{1,0:T(8,128)(2,1)} %fusion.17.v_ref, s32[1024,1]{1,0:T(8,128)} %copy.99.q_ids_ref.k_ids_ref, s32[1,1024]{1,0:T(1,128)} %k_ids_ref.3), custom_call_target="tpu_custom_call" | custom-call | tf_op jit(solution)/shard_map/pallas_call | solution.py:296
  297.9 4.0 fusion.75
  301.9 1.6 copy-done.11
  304.0 38.0 %multiply_convert_fusion = (bf16[1024,3072]{1,0:T(8,128)(2,1)S(1)}, f32[1024,3072]{1,0:T(8,128)}, f32[1024,3072]{1,0:T(8,128)}) fusion(f32[3072]{0:T(1024)S(1)} %add.246, bf16[3072,768]{1,0:T(8,128)(2,1)} %bitcast.112, f32[1024,768]{0,1:T(8,128)} %copy-done.11, f32[768]{0:T(1024)S(1)} %copy-done.60, f32[768]{0:T(1024)S(1)} %copy-done.51, ...), kind=kOutput, calls=%fused_computation.3 | convolution fusion | flops 5043388416 | bytes 39348224 | tf_op jit(solution)/shard_map/dot_general | solution.py:24
  342.0 7.5 %fusion.76 = (f32[1024]{0:T(1024)S(1)}, f32[1024,768]{0,1:T(8,128)}) fusion(f32[768]{0:T(1024)S(1)} %copy-done.59, bf16[1024,3072]{1,0:T(8,128)(2,1)S(1)} %get-tuple-element.152, bf16[3072,768]{1,0:T(8,128)(2,1)S(1)} %bitcast.117, f32[768]{0:T(1024)S(1)} %copy-done.60, f32[768]{0:T(1024)S(1)} %copy-done.51, f32[1024]{0:T(1024)S(1)} %fusion.56, ...), kind=kOutput, calls=%fused_computation.169 | convolution fusion | flops 4837342208 | bytes 17323008 | tf_op jit(solution)/shard_map/dot_general | solution.py:20
  349.6 1.7 copy.103
  351.3 3.1 fusion.8
  354.5 1.6 fusion.9
  356.1 3.0 convert_reduce_fusion.1
  359.1 18.8 %add_convert_fusion = bf16[1024,3072]{1,0:T(8,128)(2,1)} fusion(f32[1024,3072]{1,0:T(8,128)} %get-tuple-element.153, f32[1024,3072]{1,0:T(8,128)} %get-tuple-element.199, f32[3072]{0:T(1024)S(1)} %add.246, bf16[1024,768]{0,1:T(8,128)(2,1)} %get-tuple-element.145, bf16[3072,768]{1,0:T(8,128)(2,1)} %bitcast.114), kind=kOutput, calls=%fused_computation.2 | convolution fusion | flops 4879024128 | bytes 37761024 | tf_op jit(solution)/shard_map/dot_general | solution.py:24
  377.9 11.2 %multiply_reduce_fusion = (f32[768]{0:T(1024)S(1)}, f32[1024]{0:T(1024)S(1)}, f32[768]{0:T(1024)S(1)}, f32[1024,768]{0,1:T(8,128)S(1)}) fusion(f32[1024,768]{0,1:T(8,128)} %copy-done.11, f32[1024]{0:T(1024)S(1)} %fusion.56, f32[1024]{0:T(1024)S(1)} %broadcast_multiply_fusion.1, f32[768]{0:T(1024)S(1)} %copy-done.51, ...), kind=kOutput, calls=%fused_computation.29 | convolution fusion | flops 4845204480 | bytes 22061056 | tf_op jit(solution)/shard_map/dot_general | solution.py:20
  390.4 1.8 copy-done.32
  392.1 2.6 convolution_convert_fusion.1.gm_ref
  395.8 45.0 %shard_map.487 = (bf16[1024,768]{1,0:T(8,128)(2,1)}, bf16[1024,768]{1,0:T(8,128)(2,1)}, bf16[1024,768]{1,0:T(8,128)(2,1)}) custom-call(bf16[1024,768]{1,0:T(8,128)(2,1)} %add_convert_fusion.3.q_ref, bf16[1024,768]{1,0:T(8,128)(2,1)} %fusion.14.k_ref, bf16[1024,768]{1,0:T(8,128)(2,1)} %fusion.17.v_ref, bf16[1024,768]{1,0:T(8,128)(2,1)} %convolution_convert_fusion.1.gm_ref, ...), custom_call_target="tpu_custom_call" | custom-call | tf_op jit(solution)/shard_map/pallas_call | solution.py:354
  440.9 5.6 fusion.65
  446.6 1.3 multiply_reduce_fusion.1
  448.9 1.7 copy-done.9
  450.6 2.6 convolution_convert_fusion.gm_ref
  453.2 29.4 %shard_map.488 = (bf16[1024,768]{1,0:T(8,128)(2,1)}, bf16[1024,768]{1,0:T(8,128)(2,1)}, bf16[1024,768]{1,0:T(8,128)(2,1)}) custom-call(bf16[1024,768]{1,0:T(8,128)(2,1)} %fusion.15.q_ref, bf16[1024,768]{1,0:T(8,128)(2,1)} %fusion.13.k_ref, bf16[1024,768]{1,0:T(8,128)(2,1)} %fusion.16.v_ref, bf16[1024,768]{1,0:T(8,128)(2,1)} %convolution_convert_fusion.gm_ref, ...), custom_call_target="tpu_custom_call" | custom-call | tf_op jit(solution)/shard_map/pallas_call | solution.py:354
  482.6 2.6 fusion.23
  485.2 2.7 fusion.22
  488.0 2.7 fusion.21
  490.7 2.8 convolution_dynamic-update-slice_fusion.4
  493.4 2.8 convolution_dynamic-update-slice_fusion.3
  496.2 2.7 fusion.20
  498.9 2.6 fusion.19
  501.6 2.8 convolution_dynamic-update-slice_fusion.2
  504.4 5.6 convolution_dynamic-update-slice_fusion.1
  510.0 4.3 convolution_dynamic-update-slice_fusion
  514.3 9.7 %copy.120 = f32[768,3072]{1,0:T(8,128)} copy(f32[768,3072]{0,1:T(8,128)} %convolution_dynamic-update-slice_fusion) | data formatting | bytes 18874368
  524.0 1.4 copy-done.16
  525.4 1.6 copy.106
  526.9 1.9 convert_reduce_fusion.5
  528.9 1.8 convert_reduce_fusion.7
  530.7 2.0 convert_reduce_fusion.2
  532.8 23.0 %psum.7 = f32[8448]{0:T(1024)S(1)} all-reduce(f32[8448]{0:T(1024)S(1)} %concatenate.19), channel_id=1, replica_groups=mesh['dp'=8,'tensor'=4] {'dp'}, use_global_device_ids=true, to_apply=%region_27.28 | all-reduce | flops 8448 | bytes 67584 | tf_op jit(solution)/shard_map/psum | solution.py:555
  557.1 2.5 fusion.35
  559.6 2.2 convolution_add_fusion.3
  561.8 2.8 fusion.25
  564.6 1.8 convolution_add_fusion.2
  566.5 2.6 fusion.24
  569.1 33.9 %reduce-scatter.4.cloned.1.call-done = f32[96,3072]{1,0:T(8,128)} async-done(((f32[768,3072]{1,0:T(8,128)}), f32[96,3072]{1,0:T(8,128)}) %reduce-scatter.4.cloned.1.call-update) | async-done | bytes 1179664
  603.0 2.2 fusion.70
  606.7 1.9 slice_bitcast_fusion
  (171 shorter events, 19.9 us)
Async XLA Ops:
  7.2 255.9 %copy-start = (bf16[1024,768]{1,0:T(8,128)(2,1)S(1)}, bf16[1024,768]{1,0:T(8,128)(2,1)}, u32[]{:S(2)}) copy-start(bf16[1024,768]{1,0:T(8,128)(2,1)} %param.30) | copy-start | bytes 4718596
  7.2 3.5 copy-start.34
  7.2 4.3 copy-start.35
  7.2 595.8 %reduce-scatter.4.cloned.1.call-start = ((), (), s32[]{:S(2)}) async-start(), calls=%async_computation.1 | async-start | bytes 10616832
  10.7 6.5 %copy-start.36 = (bf16[768,192]{0,1:T(8,128)(2,1)S(1)}, bf16[768,192]{0,1:T(8,128)(2,1)}, u32[]{:S(2)}) copy-start(bf16[768,192]{0,1:T(8,128)(2,1)} %param.42) | copy-start | bytes 884740
  10.7 7.3 %copy-start.37 = (bf16[192,768]{1,0:T(8,128)(2,1)S(1)}, bf16[192,768]{1,0:T(8,128)(2,1)}, u32[]{:S(2)}) copy-start(bf16[192,768]{1,0:T(8,128)(2,1)} %param.47) | copy-start | bytes 884740
  10.7 9.1 %copy-start.33 = (bf16[768,768]{1,0:T(8,128)(2,1)S(1)}, bf16[768,768]{1,0:T(8,128)(2,1)}, u32[]{:S(2)}) copy-start(bf16[768,768]{1,0:T(8,128)(2,1)} %param.53) | copy-start | bytes 3538948
  19.9 6.6 %copy-start.52 = (f32[768]{0:T(1024)S(1)}, f32[768]{0:T(1024)}, u32[]{:S(2)}) copy-start(f32[768]{0:T(1024)} %param.52) | copy-start | bytes 9220
  19.9 6.6 %copy-start.53 = (f32[192]{0:T(256)S(1)}, f32[192]{0:T(256)}, u32[]{:S(2)}) copy-start(f32[192]{0:T(256)} %param.34) | copy-start | bytes 2308
  19.9 6.6 %copy-start.54 = (f32[192]{0:T(256)S(1)}, f32[192]{0:T(256)}, u32[]{:S(2)}) copy-start(f32[192]{0:T(256)} %param.37) | copy-start | bytes 2308
  19.9 6.7 %copy-start.55 = (f32[192]{0:T(256)S(1)}, f32[192]{0:T(256)}, u32[]{:S(2)}) copy-start(f32[192]{0:T(256)} %param.43) | copy-start | bytes 2308
  19.9 6.7 %copy-start.56 = (f32[192]{0:T(256)S(1)}, f32[192]{0:T(256)}, u32[]{:S(2)}) copy-start(f32[192]{0:T(256)} %param.46) | copy-start | bytes 2308
  26.6 2.3 copy-start.1
  214.6 8.3 %copy-start.7 = (bf16[1024,768]{1,0:T(8,128)(2,1)S(1)}, bf16[1024,768]{1,0:T(8,128)(2,1)}, u32[]{:S(2)}) copy-start(bf16[1024,768]{1,0:T(8,128)(2,1)} %param.29) | copy-start | bytes 4718596
  224.5 3.9 copy-start.44
  229.5 3.9 copy-start.26
  236.0 21.5 %copy-start.28 = (bf16[1024,768]{0,1:T(8,128)(2,1)S(1)}, bf16[1024,768]{0,1:T(8,128)(2,1)}, u32[]{:S(2)}) copy-start(bf16[1024,768]{0,1:T(8,128)(2,1)} %copy.94) | copy-start | bytes 4718596
  236.0 21.5 %copy-start.57 = (f32[768]{0:T(1024)S(1)}, f32[768]{0:T(1024)}, u32[]{:S(2)}) copy-start(f32[768]{0:T(1024)} %param.39) | copy-start | bytes 9220
  260.9 1.8 copy-start.2
  260.9 2.2 copy-start.27
  260.9 36.9 %copy-start.38 = (f32[1024]{0:T(1024)}, f32[1024]{0:T(1024)S(1)}, u32[]{:S(2)}) copy-start(f32[1024]{0:T(1024)S(1)} %broadcast_multiply_fusion.2) | copy-start | bytes 12292
  263.0 2.7 copy-start.45
  263.0 34.8 %copy-start.42 = (f32[1024]{0:T(1024)}, f32[1024]{0:T(1024)S(1)}, u32[]{:S(2)}) copy-start(f32[1024]{0:T(1024)S(1)} %fusion.55) | copy-start | bytes 12292
  263.1 2.6 copy-start.25
  265.7 2.6 copy-start.3
  265.7 2.6 copy-start.40
  265.7 2.6 copy-start.49
  268.3 1.7 copy-start.19
  272.7 25.2 %copy-start.31 = (bf16[4,192,768]{2,1,0:T(8,128)(2,1)S(1)}, bf16[4,192,768]{2,1,0:T(8,128)(2,1)}, u32[]{:S(2)}) copy-start(bf16[4,192,768]{2,1,0:T(8,128)(2,1)} %get-tuple-element.156) | copy-start | bytes 3538948
  272.7 25.2 %copy-start.58 = (f32[768]{0:T(1024)S(1)}, f32[768]{0:T(1024)}, u32[]{:S(2)}) copy-start(f32[768]{0:T(1024)} %param.48) | copy-start | bytes 9220
  297.9 44.1 %slice-start = ((s8[4718592]{0:T(1024)(128)(4,1)}), s8[524288]{0:T(1024)(128)(4,1)S(1)}, s32[]{:S(2)}) async-start(s8[4718592]{0:T(1024)(128)(4,1)} %bitcast.115), calls=%async_computation.2 | async-start | bytes 1048576
  301.9 1.6 copy-start.11
  301.9 2.0 copy-start.51
  301.9 2.0 copy-start.60
  303.9 38.1 %copy-start.12 = (f32[1024,768]{0,1:T(8,128)S(1)}, f32[1024,768]{0,1:T(8,128)}, u32[]{:S(2)}) copy-start(f32[1024,768]{0,1:T(8,128)} %copy-done.11) | copy-start | bytes 9437188
  303.9 38.1 %slice-start.1 = ((s8[4718592]{0:T(1024)(128)(4,1)}), s8[4194304]{0:T(1024)(128)(4,1)S(1)}, s32[]{:S(2)}) async-start(s8[4718592]{0:T(1024)(128)(4,1)} %bitcast.115), calls=%async_computation.3 | async-start | bytes 8388608
  304.0 38.1 %copy-start.59 = (f32[768]{0:T(1024)S(1)}, f32[768]{0:T(1024)}, u32[]{:S(2)}) copy-start(f32[768]{0:T(1024)} %param.54) | copy-start | bytes 9220
  342.0 7.6 %copy-start.61 = (bf16[1024,3072]{1,0:T(8,128)(2,1)}, bf16[1024,3072]{1,0:T(8,128)(2,1)S(1)}, u32[]{:S(2)}) copy-start(bf16[1024,3072]{1,0:T(8,128)(2,1)S(1)} %get-tuple-element.152) | copy-start | bytes 18874372
  349.6 1.7 copy-start.47
  351.3 3.2 copy-start.5
  354.4 1.7 copy-start.50
  377.9 11.2 %copy-start.13 = (f32[1024,768]{0,1:T(8,128)S(1)}, f32[1024,768]{0,1:T(8,128)}, u32[]{:S(2)}) copy-start(f32[1024,768]{0,1:T(8,128)} %copy-done.11) | copy-start | bytes 9437188
  390.0 4.8 copy-start.6
  390.0 2.1 copy-start.32
  390.4 4.4 copy-start.17
  392.1 2.6 copy-start.48
  395.8 45.0 %copy-start.20 = (bf16[4,192,768]{2,1,0:T(8,128)(2,1)S(1)}, bf16[4,192,768]{2,1,0:T(8,128)(2,1)}, u32[]{:S(2)}) copy-start(bf16[4,192,768]{2,1,0:T(8,128)(2,1)} %get-tuple-element.159) | copy-start | bytes 3538948
  395.8 45.0 %copy-start.39 = (f32[1024]{0:T(1024)S(1)}, f32[1024]{0:T(1024)}, u32[]{:S(2)}) copy-start(f32[1024]{0:T(1024)} %copy-done.38) | copy-start | bytes 12292
  395.8 45.0 %copy-start.41 = (f32[768]{0:T(1024)S(1)}, f32[768]{0:T(1024)}, u32[]{:S(2)}) copy-start(f32[768]{0:T(1024)} %param.40) | copy-start | bytes 9220
  440.9 5.6 copy-start.46
  440.9 5.7 copy-start.4
  440.9 5.7 copy-start.43
  447.8 2.8 copy-start.30
  448.9 1.7 copy-start.9
  453.2 29.4 %copy-start.8 = (bf16[1024,768]{1,0:T(8,128)(2,1)S(1)}, bf16[1024,768]{1,0:T(8,128)(2,1)}, u32[]{:S(2)}) copy-start(bf16[1024,768]{1,0:T(8,128)(2,1)} %param.29) | copy-start | bytes 4718596
  485.2 5.5 copy-start.10
  487.9 5.5 copy-start.15
  496.2 5.3 copy-start.18
  504.4 5.6 copy-start.29
  524.0 1.4 copy-start.16
  526.9 32.6 %copy-start.23 = (bf16[1024,768]{1,0:T(8,128)(2,1)S(1)}, bf16[1024,768]{1,0:T(8,128)(2,1)}, u32[]{:S(2)}) copy-start(bf16[1024,768]{1,0:T(8,128)(2,1)} %get-tuple-element.46) | copy-start | bytes 4718596
  557.1 4.7 copy-start.21
  559.5 5.1 copy-start.24
  561.8 4.7 copy-start.22
  (1 other events, 1.2 us)
Sparse Core Ops, SparseCore 0:
  524.1 78.8 reduce-scatter.3
